TPU v7x, 32 devices: a whole 2x2x4 slice. The times are simulated.
32 devices in a mesh: groups: 2 (over y), frame: 4 (over z), tensor: 4 (over x, core).
Axes of the slice: x: 2, y: 2, z: 4, core: 2. Of those that a mesh axis runs over, the one named last changes fastest.
Arguments:
- latent: bfloat16 [6, 1024, 1024], P(None, ('groups', 'frame')), parts along dimension 1, may hold values from -17 to 17
- norm1_gain: float32 [1024], replicated, may hold values from 0.1 to 1.9
- conv1_weight: bfloat16 [3, 1024, 1024], P(None, None, 'tensor'), may hold values from -0.109375 to 0.109375
- time_bias: float32 [1024], P('tensor'), may hold values from -4 to 4
- norm2_gain: float32 [1024], P('tensor'), may hold values from 0.1 to 1.9
- conv2_weight: bfloat16 [3, 1024, 1024], P(None, 'tensor'), may hold values from -0.375 to 0.375
- attn_gain: float32 [1024], replicated, may hold values from 0.1 to 1.9
- qkv_weight: bfloat16 [1024, 3, 1024], P(None, None, 'tensor'), may hold values from -2 to 2
- out_weight: bfloat16 [1024, 1024], P('tensor'), may hold values from -0.1875 to 0.1875
Outputs:
- velocity: bfloat16 [6, 1024, 1024], P(None, ('groups', 'frame'), 'tensor'), parts along dimension 1
There are 2 independent parts, one for each index of `groups`. A program takes and returns all parts, laid end to end along the dimension named above; an argument that names none is the same for every part. Nothing has to cross between parts.
All inputs are finite; a program needn't handle non-finite values.
Results may differ from a plain program's by a relative error of at most 0.014.
Values may be sent and summed in bfloat16 or wider, within the bound.
No kernel may reach another device: no remote copies, remote signals or barrier semaphores. Data moves between devices by JAX's collectives and lax.ppermute only.
A program may use at most 64 MiB of HBM per device.

v0:
```python
import math
import jax
import jax.numpy as jnp
from jax import lax
from jax.sharding import PartitionSpec as P

GROUPS = 32
HEAD_DIM = 64
WINDOW = 64
norm_eps = 1e-05
rms_eps = 1e-06


def extended(block, sides, width):
    for axis, dim in sides:
        count = lax.axis_size(axis)
        forward = [(i, i + 1) for i in range(count - 1)]
        backward = [(target, source) for source, target in forward]
        low = lax.ppermute(
            lax.slice_in_dim(block, block.shape[dim] - width, None, axis=dim), axis, forward
        )
        high = lax.ppermute(lax.slice_in_dim(block, 0, width, axis=dim), axis, backward)
        block = jnp.concatenate([low, block, high], axis=dim)
    return block


def group_sums(hidden, group_count):
    stem_count, frame_count, channels = hidden.shape
    grouped = hidden.reshape(stem_count, frame_count, group_count, channels // group_count)
    return (jnp.sum(grouped, axis=(1, 3)), jnp.sum(grouped * grouped, axis=(1, 3)))


def apply_group(hidden, totals, squares, entries, gain_vec):
    stem_count, frame_count, channels = hidden.shape
    group_count = totals.shape[1]
    centre = totals / entries
    spread = squares / entries - centre * centre
    grouped = hidden.reshape(stem_count, frame_count, group_count, channels // group_count)
    scaled = (grouped - centre[:, None, :, None]) * lax.rsqrt(spread + norm_eps)[:, None, :, None]
    return scaled.reshape(stem_count, frame_count, channels) * gain_vec


def conv_padded(padded, kernel, frame_count):
    stem_count = padded.shape[0]
    channels = padded.shape[2]
    result = jnp.zeros((stem_count * frame_count, kernel.shape[2]), jnp.float32)
    for tap_index in range(3):
        tap_rows = padded[:, tap_index : tap_index + frame_count].reshape(
            stem_count * frame_count, channels
        )
        result = result + jnp.dot(tap_rows, kernel[tap_index], preferred_element_type=jnp.float32)
    return result.reshape(stem_count, frame_count, kernel.shape[2])


def attend(queries, keys_all, values):
    stem_count, frame_count, head_count, head_dim = queries.shape
    window_count = frame_count // WINDOW

    def arrange(source):
        shaped = source.reshape(stem_count, window_count, WINDOW, head_count, head_dim)
        return shaped.transpose(1, 3, 0, 2, 4).reshape(
            window_count, head_count, stem_count * WINDOW, head_dim
        )

    scores = jnp.einsum(
        "nhqd,nhkd->nhqk",
        arrange(queries),
        arrange(keys_all),
        precision=lax.Precision.HIGHEST,
        preferred_element_type=jnp.float32,
    ) / math.sqrt(head_dim)
    scores = scores - jnp.max(scores, axis=3, keepdims=True)
    exp_scores = jnp.exp(scores)
    attn_probs = (exp_scores / jnp.sum(exp_scores, axis=3, keepdims=True)).astype(jnp.bfloat16)
    context = jnp.einsum(
        "nhqk,nhkd->nhqd", attn_probs, arrange(values), preferred_element_type=jnp.float32
    ).astype(jnp.bfloat16)
    context = context.reshape(window_count, head_count, stem_count, WINDOW, head_dim).transpose(
        2, 0, 3, 1, 4
    )
    return context.reshape(stem_count * frame_count, head_count * head_dim)


def local(
    latent,
    norm1_gain,
    conv1_weight,
    time_bias,
    norm2_gain,
    conv2_weight,
    attn_gain,
    qkv_weight,
    out_weight,
):
    stem_count, frame_count, channels = latent.shape
    tensor_size = lax.axis_size("tensor")
    shard_width = channels // tensor_size
    row_count = stem_count * frame_count
    group_entries = frame_count * lax.axis_size("frame") * (channels // GROUPS)
    latent_f = latent.astype(jnp.float32)
    sums_one, squares_one = group_sums(latent_f, GROUPS)
    sums_one, squares_one = lax.psum((sums_one, squares_one), "frame")
    act_one = jax.nn.silu(
        apply_group(latent_f, sums_one, squares_one, group_entries, norm1_gain)
    ).astype(jnp.bfloat16)
    padded_one = extended(act_one, (("frame", 1),), 1)
    hid_one = conv_padded(padded_one, conv1_weight, frame_count)
    hid_one = hid_one + time_bias
    local_groups = GROUPS // tensor_size
    sums_two, squares_two = group_sums(hid_one, local_groups)
    sums_two, squares_two = lax.psum((sums_two, squares_two), "frame")
    act_two = jax.nn.silu(
        apply_group(hid_one, sums_two, squares_two, group_entries, norm2_gain)
    ).astype(jnp.bfloat16)
    padded_two = extended(act_two, (("frame", 1),), 1)
    conv_term = conv_padded(padded_two, conv2_weight, frame_count)
    own_start = lax.axis_index("tensor") * shard_width
    qkv_flat = qkv_weight.reshape(channels, 3 * shard_width)
    conv_total = lax.psum(conv_term.astype(jnp.bfloat16), "tensor").astype(jnp.float32)
    residual = (latent_f + conv_total).astype(jnp.bfloat16)
    res_f = residual.astype(jnp.float32)
    mean_sq = jnp.mean(res_f * res_f, axis=2, keepdims=True)
    normed = (res_f * lax.rsqrt(mean_sq + rms_eps) * attn_gain).astype(jnp.bfloat16)
    projected = jnp.dot(
        normed.reshape(row_count, channels), qkv_flat, preferred_element_type=jnp.float32
    )
    res_own = lax.dynamic_slice_in_dim(res_f, own_start, shard_width, 2)
    head_local = shard_width // HEAD_DIM
    projected = projected.reshape(stem_count, frame_count, 3, head_local, HEAD_DIM)
    values = projected[:, :, 2].astype(jnp.bfloat16)
    context = attend(projected[:, :, 0], projected[:, :, 1], values)
    out_term = jnp.dot(context, out_weight, preferred_element_type=jnp.float32).reshape(
        stem_count, frame_count, channels
    )
    attn_share = lax.psum_scatter(
        out_term.astype(jnp.bfloat16), "tensor", scatter_dimension=2, tiled=True
    ).astype(jnp.float32)
    velocity = (res_own + attn_share).astype(jnp.bfloat16)
    return velocity


def solution(mesh):
    return jax.shard_map(
        local,
        mesh=mesh,
        in_specs=(
            P(None, ("groups", "frame"), None),
            P(),
            P(None, None, "tensor"),
            P("tensor"),
            P("tensor"),
            P(None, "tensor", None),
            P(),
            P(None, None, "tensor"),
            P("tensor", None),
        ),
        out_specs=P(None, ("groups", "frame"), "tensor"),
        check_vma=False,
    )
```

profile of v0, /device:TPU:0, one launch (start us, length us, event | category | flops | bytes accessed | tf_op | source)
XLA Modules:
  0.0 182.4 jit_solution(185818736089615130)
XLA Ops:
  6.5 2.0 %convert_reduce_fusion = (f32[6,1024]{1,0:T(8,128)S(1)}, f32[6,1024]{1,0:T(8,128)S(1)}) fusion(bf16[6,128,1024]{2,1,0:T(8,128)(2,1)} %param.9), kind=kLoop, calls=%fused_computation.4 | loop fusion | flops 3133440 | bytes 1622016 | tf_op jit(solution)/shard_map/reduce_sum | solution.py:30
  9.0 13.7 %all-reduce.1 = (f32[6,32]{1,0:T(8,128)S(1)}, f32[6,32]{1,0:T(8,128)S(1)}) all-reduce(f32[6,32]{1,0:T(8,128)S(1)} %reduce_sum.73, f32[6,32]{1,0:T(8,128)S(1)} %reduce_sum.70), channel_id=1, replica_groups=mesh['groups'=2,'frame'=4,'tensor'=4] {'frame'}, use_global_device_ids=true, to_apply=%region_5.6 | all-reduce | flops 384 | bytes 3072 | tf_op jit(solution)/shard_map/psum | solution.py:102
  23.1 2.8 %fusion.11 = bf16[6,128,1024]{2,1,0:T(8,128)(2,1)} fusion(bf16[6,128,1024]{2,1,0:T(8,128)(2,1)S(1)} %copy-done.1, f32[1024]{0:T(1024)} %param.10, f32[6,1024]{1,0:T(8,128)S(1)} %mul.101, f32[6,1024]{1,0:T(8,128)S(1)} %sub.46), kind=kLoop, calls=%fused_computation.16 | loop fusion | flops 7077888 | bytes 3198976 | tf_op jit(solution)/shard_map/convert_element_type | solution.py:105
  26.0 1.0 fusion.55
  27.0 1.3 collective-permute-start
  28.3 1.3 collective-permute-start.1
  29.6 3.0 %fusion.36 = f32[768,256]{1,0:T(8,128)} fusion(bf16[768,1024]{1,0:T(8,128)(2,1)} %bitcast.2, bf16[3,1024,256]{2,1,0:T(8,128)(2,1)} %param.11), kind=kOutput, calls=%fused_computation.56 | convolution fusion | flops 402653184 | bytes 2883584 | tf_op jit(solution)/shard_map/dot_general | solution.py:51
  32.6 1.3 collective-permute-done.1
  34.0 3.0 %pad_maximum_fusion.1 = (bf16[6,128,1024]{2,1,0:T(8,128)(2,1)S(1)}, bf16[6,128,1024]{2,1,0:T(8,128)(2,1)S(1)}) fusion(bf16[6,128,1024]{2,1,0:T(8,128)(2,1)} %fusion.11, bf16[6,1,1024]{2,1,0:T(2,128)(2,1)S(1)} %collective-permute-done, bf16[6,1,1024]{2,1,0:T(2,128)(2,1)S(1)} %collective-permute-done.1), kind=kLoop, calls=%fused_computation.31 | loop fusion | flops 6291456 | bytes 4743168 | tf_op jit(solution)/shard_map/concatenate | solution.py:23
  37.0 0.6 fusion.34
  37.6 0.6 fusion.22
  38.2 1.2 copy.37
  39.4 2.2 %reshape.92 = f32[6,128,8,32]{1,0,3,2:T(8,128)} reshape(f32[768,256]{0,1:T(8,128)} %copy.37) | data formatting | bytes 1572864 | tf_op jit(solution)/shard_map/reshape | solution.py:52
  41.7 1.6 add_reduce_fusion
  43.3 10.4 %all-reduce = (f32[6,8]{0,1:T(8,128)S(1)}, f32[6,8]{0,1:T(8,128)S(1)}) all-reduce(f32[6,8]{0,1:T(8,128)S(1)} %get-tuple-element.8, f32[6,8]{0,1:T(8,128)S(1)} %get-tuple-element.7), channel_id=1, replica_groups=mesh['groups'=2,'frame'=4,'tensor'=4] {'frame'}, use_global_device_ids=true, to_apply=%region_9.10 | all-reduce | flops 96 | bytes 768 | tf_op jit(solution)/shard_map/psum | solution.py:111
  54.2 0.3 multiply_convert_fusion.1
  54.5 0.3 multiply_convert_fusion.2
  54.7 1.4 collective-permute-start.3
  56.2 4.5 %collective-permute-start.2 = (bf16[6,1,256]{2,1,0:T(2,128)(2,1)S(1)}, bf16[6,1,256]{2,1,0:T(2,128)(2,1)S(1)}, u32[]{:S(2)}, u32[]{:S(2)}) collective-permute-start(bf16[6,1,256]{2,1,0:T(2,128)(2,1)S(1)} %get-tuple-element.24), channel_id=1, source_target_pairs={{0,4},{4,8},{8,12},{1,5},{5,9},{9,13},{2,6},{6,10},{10,14},{3,7},{... | collective-permute-start | bytes 9224 | tf_op jit(solution)/shard_map/ppermute | solution.py:19
  60.7 1.6 fusion.30
  62.4 0.2 pad_maximum_fusion.2
  62.6 0.6 fusion.32
  63.1 1.7 add_convert_fusion
  64.9 0.2 reduce-scatter.2.cloned.1.call-start
  65.1 2.6 %copy.40 = bf16[1024,3,256]{0,2,1:T(8,128)(2,1)} copy(bf16[1024,3,256]{2,0,1:T(8,128)(2,1)} %param.16) | data formatting | bytes 3145728 | tf_op args[7]
  67.7 39.7 %all-reduce.4.cloned.1.call-done = bf16[6,128,1024]{2,1,0:T(8,128)(2,1)} async-done(((bf16[6,128,1024]{2,1,0:T(8,128)(2,1)}), bf16[6,128,1024]{2,1,0:T(8,128)(2,1)}) %all-reduce.4.cloned.1.call-update) | async-done | bytes 1572880 | tf_op jit(solution)/shard_map/psum | solution.py:119
  107.5 3.7 %fusion.19 = (f32[6,128,1024]{2,1,0:T(8,128)}, f32[6,128]{1,0:T(8,128)S(1)}) fusion(bf16[6,128,1024]{2,1,0:T(8,128)(2,1)} %all-reduce.4.cloned.1.call-done, bf16[6,128,1024]{2,1,0:T(8,128)(2,1)S(1)} %copy-done.1), kind=kLoop, calls=%fused_computation.29 | loop fusion | flops 5504256 | bytes 6294528 | tf_op jit(solution)/shard_map/convert_element_type | solution.py:121
  111.2 1.6 fusion.17
  112.8 1.0 fusion.54
  113.8 0.3 convert_element_type.61
  114.2 0.5 copy.53
  114.7 1.4 reshape.98
  116.1 2.0 %reshape_squeeze.6 = f32[6,2,64,4,64]{2,1,4,3,0:T(2,128)} reshape(f32[6,128,1,4,64]{1,4,3,2,0:T(8,128)S(1)} %get-tuple-element.16) | data formatting | bytes 1572864 | tf_op jit(solution)/shard_map/reshape;squeeze | solution.py:60
  118.1 2.4 %copy.52 = f32[6,2,64,4,64]{2,0,4,3,1:T(8,128)S(1)} copy(f32[6,2,64,4,64]{2,1,4,3,0:T(2,128)} %reshape_squeeze.6) | data formatting | bytes 1572864 | tf_op jit(solution)/shard_map/reshape;squeeze | solution.py:60
  120.5 0.5 reshape.96
  120.9 3.2 %reshape_squeeze.7 = f32[6,2,64,4,64]{2,1,4,3,0:T(2,128)} reshape(f32[6,128,1,4,64]{1,4,3,2,0:T(8,128)} %get-tuple-element.15) | data formatting | bytes 1572864 | tf_op jit(solution)/shard_map/reshape;squeeze | solution.py:60
  124.1 2.4 %copy.51 = f32[6,2,64,4,64]{2,0,4,3,1:T(8,128)S(1)} copy(f32[6,2,64,4,64]{2,1,4,3,0:T(2,128)} %reshape_squeeze.7) | data formatting | bytes 1572864 | tf_op jit(solution)/shard_map/reshape;squeeze | solution.py:60
  126.5 1.4 reshape.97
  127.8 5.0 %fusion.58 = f32[2,4,384,384]{2,3,1,0:T(8,128)S(1)} fusion(f32[2,4,384,64]{2,3,1,0:T(8,128)S(1)} %reshape.96, f32[2,4,384,64]{2,3,1,0:T(8,128)} %reshape.97), kind=kOutput, calls=%fused_computation.79 | convolution fusion | flops 905969664 | bytes 6291456 | tf_op jit(solution)/shard_map/nhqd,nhkd->nhqk/dot_general | solution.py:65
  132.9 2.1 %copy-done.2 = f32[2,4,384,384]{2,3,1,0:T(8,128)} copy-done((f32[2,4,384,384]{2,3,1,0:T(8,128)}, f32[2,4,384,384]{2,3,1,0:T(8,128)S(1)}, u32[]{:S(2)}) %copy-start.2) | copy-done | bytes 4718616
  135.0 1.2 fusion.57
  136.2 5.3 %fusion.23 = bf16[2,4,384,64]{2,3,1,0:T(8,128)(2,1)S(1)} fusion(bf16[2,4,384,64]{2,3,1,0:T(8,128)(2,1)S(1)} %copy-done.7, f32[2,4,384]{2,1,0:T(4,128)S(1)} %fusion.57, f32[2,4,384,384]{2,3,1,0:T(8,128)} %copy-done.2), kind=kOutput, calls=%fused_computation.36 | convolution fusion | flops 157093248 | bytes 5517312 | tf_op jit(solution)/shard_map/nhqk,nhkd->nhqd/dot_general | solution.py:75
  141.5 0.6 reshape.99
  142.1 0.8 copy.45
  142.9 0.5 dot_general.47
  143.4 1.7 convolution_convert_fusion
  145.2 28.3 %reduce-scatter.2.cloned.1.call-done = bf16[6,128,256]{2,1,0:T(8,128)(2,1)} async-done(((bf16[6,128,1024]{2,1,0:T(8,128)(2,1)}), bf16[6,128,256]{2,1,0:T(8,128)(2,1)}) %reduce-scatter.2.cloned.1.call-update) | async-done | bytes 393232 | tf_op jit(solution)/shard_map/reduce_scatter | solution.py:135
  173.4 2.1 %add_convert_fusion.1 = bf16[6,128,256]{2,1,0:T(8,128)(2,1)} fusion(bf16[6,128,256]{2,1,0:T(8,128)(2,1)} %reduce-scatter.2.cloned.1.call-done, f32[6,128,1024]{2,1,0:T(8,128)} %get-tuple-element.13, s32[]{:T(128)S(6)} %select_n.3), kind=kLoop, calls=%fused_computation.44 | loop fusion | flops 589824 | bytes 1572868 | tf_op jit(solution)/shard_map/convert_element_type | solution.py:138
  (49 shorter events, 1.5 us)
Async XLA Ops:
  6.5 136.9 %copy-start = (bf16[256,1024]{1,0:T(8,128)(2,1)S(1)}, bf16[256,1024]{1,0:T(8,128)(2,1)}, u32[]{:S(2)}) copy-start(bf16[256,1024]{1,0:T(8,128)(2,1)} %param.17) | copy-start | bytes 1572868
  6.5 16.6 %copy-start.1 = (bf16[6,128,1024]{2,1,0:T(8,128)(2,1)S(1)}, bf16[6,128,1024]{2,1,0:T(8,128)(2,1)}, u32[]{:S(2)}) copy-start(bf16[6,128,1024]{2,1,0:T(8,128)(2,1)} %param.9) | copy-start | bytes 4718596
  6.5 100.9 %all-reduce.4.cloned.1.call-start = ((), (), s32[]{:S(2)}) async-start(), calls=%async_computation.1 | async-start | bytes 3145728 | tf_op jit(solution)/shard_map/psum | solution.py:119
  23.1 9.4 %copy-start.9 = (f32[256]{0:T(256)S(1)}, f32[256]{0:T(256)}, u32[]{:S(2)}) copy-start(f32[256]{0:T(256)} %param.12) | copy-start | bytes 3076
  27.0 5.7 %collective-permute-start = (bf16[6,1,1024]{2,1,0:T(2,128)(2,1)S(1)}, bf16[6,1,1024]{2,1,0:T(2,128)(2,1)S(1)}, u32[]{:S(2)}, u32[]{:S(2)}) collective-permute-start(bf16[6,1,1024]{2,1,0:T(2,128)(2,1)S(1)} %get-tuple-element.19), channel_id=1, source_target_pairs={{0,4},{4,8},{8,12},{1,5},{5,9},{9,13},{2,6},{6,10},{10,14},{3,7},{... | collective-permute-start | bytes 36872 | tf_op jit(solution)/shard_map/ppermute | solution.py:19
  28.3 5.7 %collective-permute-start.1 = (bf16[6,1,1024]{2,1,0:T(2,128)(2,1)S(1)}, bf16[6,1,1024]{2,1,0:T(2,128)(2,1)S(1)}, u32[]{:S(2)}, u32[]{:S(2)}) collective-permute-start(bf16[6,1,1024]{2,1,0:T(2,128)(2,1)S(1)} %get-tuple-element.20), channel_id=1, source_target_pairs={{4,0},{8,4},{12,8},{5,1},{9,5},{13,9},{6,2},{10,6},{14,10},{7,3},{... | collective-permute-start | bytes 36872 | tf_op jit(solution)/shard_map/ppermute | solution.py:22
  32.6 4.4 %copy-start.8 = (bf16[3,1024,256]{2,1,0:T(8,128)(2,1)S(1)}, bf16[3,1024,256]{2,1,0:T(8,128)(2,1)}, u32[]{:S(2)}) copy-start(bf16[3,1024,256]{2,1,0:T(8,128)(2,1)} %param.11) | copy-start | bytes 4718596
  32.6 5.0 %copy-start.6 = (f32[768,256]{1,0:T(8,128)S(1)}, f32[768,256]{1,0:T(8,128)}, u32[]{:S(2)}) copy-start(f32[768,256]{1,0:T(8,128)} %fusion.36) | copy-start | bytes 2359300
  38.2 16.0 %copy-start.10 = (f32[256]{0:T(256)S(1)}, f32[256]{0:T(256)}, u32[]{:S(2)}) copy-start(f32[256]{0:T(256)} %param.13) | copy-start | bytes 3076
  54.4 8.1 %copy-start.5 = (bf16[3,256,1024]{2,1,0:T(8,128)(2,1)S(1)}, bf16[3,256,1024]{2,1,0:T(8,128)(2,1)}, u32[]{:S(2)}) copy-start(bf16[3,256,1024]{2,1,0:T(8,128)(2,1)} %param.14) | copy-start | bytes 4718596
  54.7 7.6 %collective-permute-start.3 = (bf16[6,1,256]{2,1,0:T(2,128)(2,1)S(1)}, bf16[6,1,256]{2,1,0:T(2,128)(2,1)S(1)}, u32[]{:S(2)}, u32[]{:S(2)}) collective-permute-start(bf16[6,1,256]{2,1,0:T(2,128)(2,1)S(1)} %get-tuple-element.23), channel_id=1, source_target_pairs={{4,0},{8,4},{12,8},{5,1},{9,5},{13,9},{6,2},{10,6},{14,10},{7,3},{... | collective-permute-start | bytes 9224 | tf_op jit(solution)/shard_map/ppermute | solution.py:22
  56.2 6.2 %collective-permute-start.2 = (bf16[6,1,256]{2,1,0:T(2,128)(2,1)S(1)}, bf16[6,1,256]{2,1,0:T(2,128)(2,1)S(1)}, u32[]{:S(2)}, u32[]{:S(2)}) collective-permute-start(bf16[6,1,256]{2,1,0:T(2,128)(2,1)S(1)} %get-tuple-element.24), channel_id=1, source_target_pairs={{0,4},{4,8},{8,12},{1,5},{5,9},{9,13},{2,6},{6,10},{10,14},{3,7},{... | collective-permute-start | bytes 9224 | tf_op jit(solution)/shard_map/ppermute | solution.py:19
  64.9 108.5 %reduce-scatter.2.cloned.1.call-start = ((), (), s32[]{:S(2)}) async-start(), calls=%async_computation.2 | async-start | bytes 1966080 | tf_op jit(solution)/shard_map/reduce_scatter | solution.py:135
  67.7 43.5 %copy-start.11 = (f32[1024]{0:T(1024)S(1)}, f32[1024]{0:T(1024)}, u32[]{:S(2)}) copy-start(f32[1024]{0:T(1024)} %param.15) | copy-start | bytes 12292
  107.4 3.7 %copy-start.3 = (bf16[1024,3,256]{0,2,1:T(8,128)(2,1)S(1)}, bf16[1024,3,256]{0,2,1:T(8,128)(2,1)}, u32[]{:S(2)}) copy-start(bf16[1024,3,256]{0,2,1:T(8,128)(2,1)} %copy.40) | copy-start | bytes 4718596
  107.4 3.7 %copy-start.4 = (bf16[6,128,1024]{2,1,0:T(8,128)(2,1)S(1)}, bf16[6,128,1024]{2,1,0:T(8,128)(2,1)}, u32[]{:S(2)}) copy-start(bf16[6,128,1024]{2,1,0:T(8,128)(2,1)} %all-reduce.4.cloned.1.call-done) | copy-start | bytes 4718596
  132.9 2.1 %copy-start.2 = (f32[2,4,384,384]{2,3,1,0:T(8,128)}, f32[2,4,384,384]{2,3,1,0:T(8,128)S(1)}, u32[]{:S(2)}) copy-start(f32[2,4,384,384]{2,3,1,0:T(8,128)S(1)} %fusion.58) | copy-start | bytes 14155780
  135.0 1.2 copy-start.7
Sparse Core Ops, SparseCore 0:
  65.0 42.3 all-reduce.3
  145.3 28.0 reduce-scatter.1
where the time goes:
time: 183 us; the launch traced here: 182 us
  waiting for transfers between devices  69.4 us (38%)
  local copies, waits for them, and re-layouts  27.2 us (15%)
  blocking collectives  24.1 us (13%)
  matrix products  21.7 us (12%)
  other arithmetic  17.4 us (10%)
  between operations  13.8 us (8%)
  starting transfers between devices  8.78 us (5%)
    psum x1, waiting for transfers between devices, local(): lax.psum(conv_term.astype(jnp.bfloat16), 'tensor').astype(jnp.float32)  39.7 us
    reduce_scatter x1, waiting for transfers between devices, local(): lax.psum_scatter(out_term.astype(jnp.bfloat16), 'tensor', scatter_dimensi...  28.3 us
    psum x1, blocking collectives, local(): sums_one, squares_one = lax.psum((sums_one, squares_one), 'frame')  13.7 us
    psum x1, blocking collectives, local(): sums_two, squares_two = lax.psum((sums_two, squares_two), 'frame')  10.4 us
    another operation x4, local copies, waits for them, and re-layouts, arrange(): source.reshape(stem_count, window_count, WINDOW, head_count, head_dim)  9.92 us
    dot_general x6, matrix products, conv_padded(): jnp.dot(tap_rows, kernel[tap_index], preferred_element_type=jnp.float32)  8.07 us
    ppermute x2, starting transfers between devices, extended(): lax.ppermute(lax.slice_in_dim(block, block.shape[dim] - width, None, axis...  5.84 us
    dot_general x1, matrix products, attend(): jnp.einsum('nhqk,nhkd->nhqd', attn_probs, arrange(values), preferred_elem...  5.34 us
  transfers between devices with their start and end apart: 6, of which 3 were waited for; matrix products, arithmetic and copies ran while one was open for 4% of the time, Pallas kernels for 0%

commit v1 on v0

--- a/solution.py
+++ b/solution.py
@@ -116,7 +116,9 @@
     conv_term = conv_padded(padded_two, conv2_weight, frame_count)
     own_start = lax.axis_index("tensor") * shard_width
     qkv_flat = qkv_weight.reshape(channels, 3 * shard_width)
-    conv_total = lax.psum(conv_term.astype(jnp.bfloat16), "tensor").astype(jnp.float32)
+    conv_total = jnp.sum(lax.all_gather(conv_term.astype(jnp.bfloat16), "tensor"), axis=0).astype(
+        jnp.float32
+    )
     residual = (latent_f + conv_total).astype(jnp.bfloat16)
     res_f = residual.astype(jnp.float32)
     mean_sq = jnp.mean(res_f * res_f, axis=2, keepdims=True)

time: 183 us -> 190 us (1.038)
  other arithmetic: 17.4 us -> 22.2 us
  waiting for transfers between devices: 69.4 us -> 73.3 us
    all_gather x0 -> x1, waiting for transfers between devices: none -> 43.3 us  [local(): lax.all_gather(conv_term.astype(jnp.bfloat16), 'tensor')]
    psum x1 -> x0, waiting for transfers between devices: 39.7 us -> none  [local(): lax.psum(conv_term.astype(jnp.bfloat16), 'tensor').astype(jnp.float32)]
    reduce_sum x0 -> x1, other arithmetic: none -> 5.95 us  [local(): jnp.sum(lax.all_gather(conv_term.astype(jnp.bfloat16), 'tensor'), axis=0)]
    unnamed x25 -> x27, local copies, waits for them, and re-layouts: 4.76 us -> 4.8 us
where the time goes in v1:
time: 190 us; the launch traced here: 189 us
  waiting for transfers between devices  73.3 us (39%)
  local copies, waits for them, and re-layouts  26.3 us (14%)
  blocking collectives  23.6 us (12%)
  other arithmetic  22.2 us (12%)
  matrix products  21.3 us (11%)
  between operations  13.8 us (7%)
  starting transfers between devices  8.78 us (5%)
    all_gather x1, waiting for transfers between devices, local(): lax.all_gather(conv_term.astype(jnp.bfloat16), 'tensor')  43.3 us
    reduce_scatter x1, waiting for transfers between devices, local(): lax.psum_scatter(out_term.astype(jnp.bfloat16), 'tensor', scatter_dimensi...  28.1 us
    psum x1, blocking collectives, local(): sums_one, squares_one = lax.psum((sums_one, squares_one), 'frame')  13.7 us
    another operation x4, local copies, waits for them, and re-layouts, arrange(): source.reshape(stem_count, window_count, WINDOW, head_count, head_dim)  9.92 us
    psum x1, blocking collectives, local(): sums_two, squares_two = lax.psum((sums_two, squares_two), 'frame')  9.84 us
    dot_general x6, matrix products, conv_padded(): jnp.dot(tap_rows, kernel[tap_index], preferred_element_type=jnp.float32)  7.62 us
    reduce_sum x1, other arithmetic, local(): jnp.sum(lax.all_gather(conv_term.astype(jnp.bfloat16), 'tensor'), axis=0)  5.95 us
    ppermute x2, starting transfers between devices, extended(): lax.ppermute(lax.slice_in_dim(block, block.shape[dim] - width, None, axis...  5.84 us
  transfers between devices with their start and end apart: 6, of which 3 were waited for; matrix products, arithmetic and copies ran while one was open for 4% of the time, Pallas kernels for 0%

profile of v1, /device:TPU:0, one launch (start us, length us, event | category | flops | bytes accessed | tf_op | source)
XLA Modules:
  0.0 189.2 jit_solution(4389776018996580086)
XLA Ops:
  6.5 2.0 %convert_reduce_fusion = (f32[6,1024]{1,0:T(8,128)S(1)}, f32[6,1024]{1,0:T(8,128)S(1)}) fusion(bf16[6,128,1024]{2,1,0:T(8,128)(2,1)} %param.9), kind=kLoop, calls=%fused_computation.4 | loop fusion | flops 3133440 | bytes 1622016 | tf_op jit(solution)/shard_map/reduce_sum | solution.py:30
  9.0 13.7 %all-reduce.1 = (f32[6,32]{1,0:T(8,128)S(1)}, f32[6,32]{1,0:T(8,128)S(1)}) all-reduce(f32[6,32]{1,0:T(8,128)S(1)} %reduce_sum.85, f32[6,32]{1,0:T(8,128)S(1)} %reduce_sum.82), channel_id=1, replica_groups=mesh['groups'=2,'frame'=4,'tensor'=4] {'frame'}, use_global_device_ids=true, to_apply=%region_5.6 | all-reduce | flops 384 | bytes 3072 | tf_op jit(solution)/shard_map/psum | solution.py:102
  23.1 1.7 fusion.11
  24.9 1.3 collective-permute-start
  26.2 1.3 collective-permute-start.1
  27.5 2.5 %fusion.36 = f32[768,256]{1,0:T(8,128)} fusion(bf16[768,1024]{1,0:T(8,128)(2,1)S(1)} %bitcast.102, bf16[3,1024,256]{2,1,0:T(8,128)(2,1)} %param.11), kind=kOutput, calls=%fused_computation.56 | convolution fusion | flops 402653184 | bytes 2883584 | tf_op jit(solution)/shard_map/dot_general | solution.py:51
  30.1 1.8 collective-permute-done.1
  31.9 3.0 %pad_maximum_fusion.1 = (bf16[6,128,1024]{2,1,0:T(8,128)(2,1)S(1)}, bf16[6,128,1024]{2,1,0:T(8,128)(2,1)S(1)}) fusion(bf16[6,128,1024]{2,1,0:T(8,128)(2,1)} %copy-done.2, bf16[6,1,1024]{2,1,0:T(2,128)(2,1)S(1)} %collective-permute-done, bf16[6,1,1024]{2,1,0:T(2,128)(2,1)S(1)} %collective-permute-done.1), kind=kLoop, calls=%fused_computation.31 | loop fusion | flops 6291456 | bytes 4743168 | tf_op jit(solution)/shard_map/concatenate | solution.py:23
  35.0 0.6 fusion.34
  35.6 0.6 fusion.22
  36.2 1.2 copy.37
  37.4 2.2 %reshape.102 = f32[6,128,8,32]{1,0,3,2:T(8,128)} reshape(f32[768,256]{0,1:T(8,128)} %copy.37) | data formatting | bytes 1572864 | tf_op jit(solution)/shard_map/reshape | solution.py:52
  39.6 1.6 add_reduce_fusion
  41.2 9.8 %all-reduce = (f32[6,8]{0,1:T(8,128)S(1)}, f32[6,8]{0,1:T(8,128)S(1)}) all-reduce(f32[6,8]{0,1:T(8,128)S(1)} %get-tuple-element.8, f32[6,8]{0,1:T(8,128)S(1)} %get-tuple-element.7), channel_id=1, replica_groups=mesh['groups'=2,'frame'=4,'tensor'=4] {'frame'}, use_global_device_ids=true, to_apply=%region_9.10 | all-reduce | flops 96 | bytes 768 | tf_op jit(solution)/shard_map/psum | solution.py:111
  51.6 0.3 multiply_convert_fusion.1
  51.9 0.3 multiply_convert_fusion.2
  52.1 1.4 collective-permute-start.3
  53.6 4.5 %collective-permute-start.2 = (bf16[6,1,256]{2,1,0:T(2,128)(2,1)S(1)}, bf16[6,1,256]{2,1,0:T(2,128)(2,1)S(1)}, u32[]{:S(2)}, u32[]{:S(2)}) collective-permute-start(bf16[6,1,256]{2,1,0:T(2,128)(2,1)S(1)} %get-tuple-element.24), channel_id=1, source_target_pairs={{0,4},{4,8},{8,12},{1,5},{5,9},{9,13},{2,6},{6,10},{10,14},{3,7},{... | collective-permute-start | bytes 9224 | tf_op jit(solution)/shard_map/ppermute | solution.py:19
  58.1 1.6 fusion.30
  59.8 0.2 pad_maximum_fusion.2
  60.0 0.6 fusion.32
  60.6 1.7 add_convert_fusion
  62.3 0.2 reduce-scatter.2.cloned.1.call-start
  62.5 2.6 %copy.40 = bf16[1024,3,256]{0,2,1:T(8,128)(2,1)} copy(bf16[1024,3,256]{2,0,1:T(8,128)(2,1)} %param.16) | data formatting | bytes 3145728 | tf_op args[7]
  65.2 43.3 %all-gather.2.cloned.1.call-done = bf16[4,6,128,1024]{3,2,1,0:T(8,128)(2,1)} async-done(((bf16[1,6,128,1024]{3,2,1,0:T(8,128)(2,1)}), bf16[4,6,128,1024]{3,2,1,0:T(8,128)(2,1)}) %all-gather.2.cloned.1.call-update) | async-done | bytes 6291472 | tf_op jit(solution)/shard_map/all_gather | solution.py:119
  108.5 6.0 %reduce_sum.88 = bf16[6,128,1024]{2,1,0:T(8,128)(2,1)} reduce(bf16[4,6,128,1024]{3,2,1,0:T(8,128)(2,1)} %all-gather.2.cloned.1.call-done, bf16[]{:T(256)} %constant.11.clone.1), dimensions={0}, to_apply=%region_10.11 | reduce | flops 2359296 | bytes 7864322 | tf_op jit(solution)/shard_map/reduce_sum | solution.py:119
  114.4 3.7 %fusion.19 = (f32[6,128,1024]{2,1,0:T(8,128)}, f32[6,128]{1,0:T(8,128)S(1)}) fusion(bf16[6,128,1024]{2,1,0:T(8,128)(2,1)} %reduce_sum.88, bf16[6,128,1024]{2,1,0:T(8,128)(2,1)S(1)} %copy-done.1), kind=kLoop, calls=%fused_computation.29 | loop fusion | flops 5504256 | bytes 6294528 | tf_op jit(solution)/shard_map/convert_element_type | solution.py:123
  118.2 1.6 fusion.17
  119.8 1.0 fusion.54
  120.8 0.3 convert_element_type.70
  121.1 0.5 copy.53
  121.7 1.4 reshape.108
  123.0 2.0 %reshape_squeeze.6 = f32[6,2,64,4,64]{2,1,4,3,0:T(2,128)} reshape(f32[6,128,1,4,64]{1,4,3,2,0:T(8,128)S(1)} %get-tuple-element.16) | data formatting | bytes 1572864 | tf_op jit(solution)/shard_map/reshape;squeeze | solution.py:60
  125.1 2.4 %copy.52 = f32[6,2,64,4,64]{2,0,4,3,1:T(8,128)S(1)} copy(f32[6,2,64,4,64]{2,1,4,3,0:T(2,128)} %reshape_squeeze.6) | data formatting | bytes 1572864 | tf_op jit(solution)/shard_map/reshape;squeeze | solution.py:60
  127.4 0.5 reshape.106
  127.9 3.2 %reshape_squeeze.7 = f32[6,2,64,4,64]{2,1,4,3,0:T(2,128)} reshape(f32[6,128,1,4,64]{1,4,3,2,0:T(8,128)} %get-tuple-element.15) | data formatting | bytes 1572864 | tf_op jit(solution)/shard_map/reshape;squeeze | solution.py:60
  131.1 2.4 %copy.51 = f32[6,2,64,4,64]{2,0,4,3,1:T(8,128)S(1)} copy(f32[6,2,64,4,64]{2,1,4,3,0:T(2,128)} %reshape_squeeze.7) | data formatting | bytes 1572864 | tf_op jit(solution)/shard_map/reshape;squeeze | solution.py:60
  133.4 1.4 reshape.107
  134.8 5.0 %fusion.58 = f32[2,4,384,384]{2,3,1,0:T(8,128)S(1)} fusion(f32[2,4,384,64]{2,3,1,0:T(8,128)S(1)} %reshape.106, f32[2,4,384,64]{2,3,1,0:T(8,128)} %reshape.107), kind=kOutput, calls=%fused_computation.79 | convolution fusion | flops 905969664 | bytes 6291456 | tf_op jit(solution)/shard_map/nhqd,nhkd->nhqk/dot_general | solution.py:65
  139.9 2.1 %copy-done.4 = f32[2,4,384,384]{2,3,1,0:T(8,128)} copy-done((f32[2,4,384,384]{2,3,1,0:T(8,128)}, f32[2,4,384,384]{2,3,1,0:T(8,128)S(1)}, u32[]{:S(2)}) %copy-start.4) | copy-done | bytes 4718616
  142.0 1.2 fusion.57
  143.1 5.3 %fusion.23 = bf16[2,4,384,64]{2,3,1,0:T(8,128)(2,1)S(1)} fusion(bf16[2,4,384,64]{2,3,1,0:T(8,128)(2,1)S(1)} %copy-done.8, f32[2,4,384]{2,1,0:T(4,128)S(1)} %fusion.57, f32[2,4,384,384]{2,3,1,0:T(8,128)} %copy-done.4), kind=kOutput, calls=%fused_computation.36 | convolution fusion | flops 157093248 | bytes 5517312 | tf_op jit(solution)/shard_map/nhqk,nhkd->nhqd/dot_general | solution.py:75
  148.5 0.6 reshape.109
  149.1 0.8 copy.45
  149.9 0.5 dot_general.47
  150.4 1.7 convolution_convert_fusion
  152.2 28.1 %reduce-scatter.2.cloned.1.call-done = bf16[6,128,256]{2,1,0:T(8,128)(2,1)} async-done(((bf16[6,128,1024]{2,1,0:T(8,128)(2,1)}), bf16[6,128,256]{2,1,0:T(8,128)(2,1)}) %reduce-scatter.2.cloned.1.call-update) | async-done | bytes 393232 | tf_op jit(solution)/shard_map/reduce_scatter | solution.py:137
  180.3 2.1 %add_convert_fusion.1 = bf16[6,128,256]{2,1,0:T(8,128)(2,1)} fusion(bf16[6,128,256]{2,1,0:T(8,128)(2,1)} %reduce-scatter.2.cloned.1.call-done, f32[6,128,1024]{2,1,0:T(8,128)} %get-tuple-element.13, s32[]{:T(128)S(6)} %select_n.3), kind=kLoop, calls=%fused_computation.44 | loop fusion | flops 589824 | bytes 1572868 | tf_op jit(solution)/shard_map/convert_element_type | solution.py:140
  (52 shorter events, 1.5 us)
Async XLA Ops:
  6.5 143.8 %copy-start = (bf16[256,1024]{1,0:T(8,128)(2,1)S(1)}, bf16[256,1024]{1,0:T(8,128)(2,1)}, u32[]{:S(2)}) copy-start(bf16[256,1024]{1,0:T(8,128)(2,1)} %param.17) | copy-start | bytes 1572868
  6.5 16.6 %copy-start.1 = (bf16[6,128,1024]{2,1,0:T(8,128)(2,1)S(1)}, bf16[6,128,1024]{2,1,0:T(8,128)(2,1)}, u32[]{:S(2)}) copy-start(bf16[6,128,1024]{2,1,0:T(8,128)(2,1)} %param.9) | copy-start | bytes 4718596
  6.5 101.9 %all-gather.2.cloned.1.call-start = ((), (), s32[]{:S(2)}) async-start(), calls=%async_computation.1 | async-start | bytes 7864320 | tf_op jit(solution)/shard_map/all_gather | solution.py:119
  23.1 6.9 %copy-start.10 = (f32[256]{0:T(256)S(1)}, f32[256]{0:T(256)}, u32[]{:S(2)}) copy-start(f32[256]{0:T(256)} %param.12) | copy-start | bytes 3076
  24.8 2.7 %copy-start.2 = (bf16[6,128,1024]{2,1,0:T(8,128)(2,1)}, bf16[6,128,1024]{2,1,0:T(8,128)(2,1)S(1)}, u32[]{:S(2)}) copy-start(bf16[6,128,1024]{2,1,0:T(8,128)(2,1)S(1)} %fusion.11) | copy-start | bytes 4718596
  24.9 5.2 %collective-permute-start = (bf16[6,1,1024]{2,1,0:T(2,128)(2,1)S(1)}, bf16[6,1,1024]{2,1,0:T(2,128)(2,1)S(1)}, u32[]{:S(2)}, u32[]{:S(2)}) collective-permute-start(bf16[6,1,1024]{2,1,0:T(2,128)(2,1)S(1)} %get-tuple-element.19), channel_id=1, source_target_pairs={{0,4},{4,8},{8,12},{1,5},{5,9},{9,13},{2,6},{6,10},{10,14},{3,7},{... | collective-permute-start | bytes 36872 | tf_op jit(solution)/shard_map/ppermute | solution.py:19
  26.2 5.7 %collective-permute-start.1 = (bf16[6,1,1024]{2,1,0:T(2,128)(2,1)S(1)}, bf16[6,1,1024]{2,1,0:T(2,128)(2,1)S(1)}, u32[]{:S(2)}, u32[]{:S(2)}) collective-permute-start(bf16[6,1,1024]{2,1,0:T(2,128)(2,1)S(1)} %get-tuple-element.20), channel_id=1, source_target_pairs={{4,0},{8,4},{12,8},{5,1},{9,5},{13,9},{6,2},{10,6},{14,10},{7,3},{... | collective-permute-start | bytes 36872 | tf_op jit(solution)/shard_map/ppermute | solution.py:22
  30.1 4.9 %copy-start.9 = (bf16[3,1024,256]{2,1,0:T(8,128)(2,1)S(1)}, bf16[3,1024,256]{2,1,0:T(8,128)(2,1)}, u32[]{:S(2)}) copy-start(bf16[3,1024,256]{2,1,0:T(8,128)(2,1)} %param.11) | copy-start | bytes 4718596
  30.1 5.5 %copy-start.7 = (f32[768,256]{1,0:T(8,128)S(1)}, f32[768,256]{1,0:T(8,128)}, u32[]{:S(2)}) copy-start(f32[768,256]{1,0:T(8,128)} %fusion.36) | copy-start | bytes 2359300
  36.1 15.4 %copy-start.11 = (f32[256]{0:T(256)S(1)}, f32[256]{0:T(256)}, u32[]{:S(2)}) copy-start(f32[256]{0:T(256)} %param.13) | copy-start | bytes 3076
  51.9 8.1 %copy-start.6 = (bf16[3,256,1024]{2,1,0:T(8,128)(2,1)S(1)}, bf16[3,256,1024]{2,1,0:T(8,128)(2,1)}, u32[]{:S(2)}) copy-start(bf16[3,256,1024]{2,1,0:T(8,128)(2,1)} %param.14) | copy-start | bytes 4718596
  52.1 7.6 %collective-permute-start.3 = (bf16[6,1,256]{2,1,0:T(2,128)(2,1)S(1)}, bf16[6,1,256]{2,1,0:T(2,128)(2,1)S(1)}, u32[]{:S(2)}, u32[]{:S(2)}) collective-permute-start(bf16[6,1,256]{2,1,0:T(2,128)(2,1)S(1)} %get-tuple-element.23), channel_id=1, source_target_pairs={{4,0},{8,4},{12,8},{5,1},{9,5},{13,9},{6,2},{10,6},{14,10},{7,3},{... | collective-permute-start | bytes 9224 | tf_op jit(solution)/shard_map/ppermute | solution.py:22
  53.6 6.2 %collective-permute-start.2 = (bf16[6,1,256]{2,1,0:T(2,128)(2,1)S(1)}, bf16[6,1,256]{2,1,0:T(2,128)(2,1)S(1)}, u32[]{:S(2)}, u32[]{:S(2)}) collective-permute-start(bf16[6,1,256]{2,1,0:T(2,128)(2,1)S(1)} %get-tuple-element.24), channel_id=1, source_target_pairs={{0,4},{4,8},{8,12},{1,5},{5,9},{9,13},{2,6},{6,10},{10,14},{3,7},{... | collective-permute-start | bytes 9224 | tf_op jit(solution)/shard_map/ppermute | solution.py:19
  62.3 118.0 %reduce-scatter.2.cloned.1.call-start = ((), (), s32[]{:S(2)}) async-start(), calls=%async_computation.2 | async-start | bytes 1966080 | tf_op jit(solution)/shard_map/reduce_scatter | solution.py:137
  114.4 3.7 %copy-start.3 = (bf16[6,128,1024]{2,1,0:T(8,128)(2,1)S(1)}, bf16[6,128,1024]{2,1,0:T(8,128)(2,1)}, u32[]{:S(2)}) copy-start(bf16[6,128,1024]{2,1,0:T(8,128)(2,1)} %reduce_sum.88) | copy-start | bytes 4718596
  114.4 3.7 %copy-start.5 = (bf16[1024,3,256]{0,2,1:T(8,128)(2,1)S(1)}, bf16[1024,3,256]{0,2,1:T(8,128)(2,1)}, u32[]{:S(2)}) copy-start(bf16[1024,3,256]{0,2,1:T(8,128)(2,1)} %copy.40) | copy-start | bytes 4718596
  114.4 3.7 %copy-start.12 = (f32[1024]{0:T(1024)S(1)}, f32[1024]{0:T(1024)}, u32[]{:S(2)}) copy-start(f32[1024]{0:T(1024)} %param.15) | copy-start | bytes 12292
  139.8 2.1 %copy-start.4 = (f32[2,4,384,384]{2,3,1,0:T(8,128)}, f32[2,4,384,384]{2,3,1,0:T(8,128)S(1)}, u32[]{:S(2)}) copy-start(f32[2,4,384,384]{2,3,1,0:T(8,128)S(1)} %fusion.58) | copy-start | bytes 14155780
  142.0 1.2 copy-start.8
Sparse Core Ops, SparseCore 0:
  62.4 45.9 all-gather.1
  152.3 27.9 reduce-scatter.1
